TPU v7x, 32 devices: a whole 2x2x4 slice. The times are simulated.
32 devices in a mesh: state: 8 (over z, y), tile: 4 (over x, core).
Axes of the slice: x: 2, y: 2, z: 4, core: 2. Of those that a mesh axis runs over, the one named last changes fastest.
Arguments:
- pair_tiles: bfloat16 [8, 4, 64, 64, 128], P('state', 'tile'), may hold values from -60 to 60
- targets: int32 [8, 4, 16, 2, 128], P('state', 'tile'), may hold values from 0 to 63, as said below
- offsets: int32 [8], replicated, may hold values from 0 to 128, as said below
- ln_gain: float32 [128], replicated, may hold values from 0.5 to 1.5
- ln_bias: float32 [128], replicated, may hold values from -3 to 3
- w_query: bfloat16 [128, 128], replicated, may hold values from -0.5 to 0.5
- w_key: bfloat16 [128, 128], replicated, may hold values from -0.5 to 0.5
- w_value: bfloat16 [128, 128], replicated, may hold values from -0.5 to 0.5
- w_pairbias: float32 [128, 4], replicated, may hold values from -25 to 25
- w_gate: bfloat16 [128, 128], replicated, may hold values from -0.5 to 0.5
- gate_bias: float32 [128], replicated, may hold values from -4 to 4
- w_output: bfloat16 [128, 128], replicated, may hold values from -0.5 to 0.5
- out_bias: float32 [128], replicated, may hold values from -3 to 3
- w_distogram: float32 [128, 64], replicated, may hold values from -4 to 4
- dist_bias: float32 [64], replicated, may hold values from -4 to 4
Outputs:
- shared_grad: float32 [4, 4, 16, 2, 128, 128], P(None, 'tile', None, None, 'state')
Inputs may be any that keep to these rules, and one draw needn't show every extreme that they name: `targets`: symmetric: the bin of crop pair (x, y) equals that of (y, x) in every state. `offsets`: each is a multiple of 64; some state starts at 0 and some state at 128.
All inputs are finite; a program needn't handle non-finite values.
Results may differ from a plain program's by a relative error of at most 0.015.
Values may be sent and summed in bfloat16 or wider, within the bound.
No kernel may reach another device: no remote copies, remote signals or barrier semaphores. Data moves between devices by JAX's collectives and lax.ppermute only.
A program may use at most 64 MiB of HBM per device.

v0:
```python
import math
import jax
import jax.numpy as jnp
from jax import lax
from jax.sharding import PartitionSpec as P

C = 128
H = 4
HD = 32
NB = 64
L = 128


def layer_norm(pair_field, ln_gain, ln_bias):
    center = pair_field - jnp.mean(pair_field, axis=-1, keepdims=True)
    inverse = lax.rsqrt(jnp.mean(center * center, axis=-1, keepdims=True) + 1e-05)
    normed = center * inverse
    return (normed * ln_gain + ln_bias, normed, inverse)


def probabilities(queries, key_proj, bias_full):
    scores = jnp.einsum("rjhd,rkhd->rhjk", queries, key_proj, preferred_element_type=jnp.float32)
    scores = scores * (1.0 / math.sqrt(HD)) + bias_full[None]
    row_max = jnp.max(scores, axis=-1, keepdims=True)
    exp_scores = jnp.exp(scores - row_max)
    return exp_scores / jnp.sum(exp_scores, axis=-1, keepdims=True)


def on_device(
    pair_tiles,
    targets,
    offsets,
    ln_gain,
    ln_bias,
    w_query,
    w_key,
    w_value,
    w_pairbias,
    w_gate,
    gate_bias,
    w_output,
    out_bias,
    w_distogram,
    dist_bias,
):
    tile_count = lax.axis_size("tile")
    state_count = lax.axis_size("state")
    tile_side = pair_tiles.shape[2]
    tile_grid = L // tile_side
    row_share = tile_side // tile_count
    rows_here = row_share * tile_grid
    hidden_width = H * HD
    inv_root = 1.0 / math.sqrt(HD)
    block_rows = 2
    groups = rows_here // block_rows

    def split_rows(values_in):
        return values_in.reshape((groups, block_rows) + values_in.shape[1:])

    blocked = pair_tiles[0, 0].reshape(tile_count, row_share, tile_side, C)
    regrouped = lax.all_to_all(blocked, "tile", split_axis=0, concat_axis=2, tiled=True)
    pair_field = regrouped.reshape(rows_here, L, C).astype(jnp.float32)
    normed_out, normed, inverse = layer_norm(pair_field, ln_gain, ln_bias)
    flat_b = normed_out.astype(jnp.bfloat16).reshape(rows_here * L, C)

    def project(weight):
        return (
            jnp.dot(flat_b, weight, preferred_element_type=jnp.float32)
            .astype(jnp.bfloat16)
            .reshape(rows_here, L, H, HD)
        )

    queries = project(w_query)
    key_proj = project(w_key)
    value_proj = project(w_value)
    gate_act = jax.nn.sigmoid(
        jnp.dot(flat_b, w_gate, preferred_element_type=jnp.float32) + gate_bias
    ).reshape(rows_here, L, hidden_width)
    bias_rows = jnp.einsum("rlc,ch->hrl", normed_out, w_pairbias, precision=lax.Precision.HIGHEST)
    gathered = lax.all_gather(bias_rows, "tile", axis=1, tiled=True)
    bias_full = (
        gathered.reshape(H, tile_count, row_share, tile_grid, L)
        .transpose(0, 3, 1, 2, 4)
        .reshape(H, L, L)
    )

    def forward_block(block_args):
        query_blk, key_blk, value_blk = block_args
        weights_b = probabilities(query_blk, key_blk, bias_full).astype(jnp.bfloat16)
        return jnp.einsum(
            "rhjk,rkhd->rjhd", weights_b, value_blk, preferred_element_type=jnp.float32
        )

    attended = lax.map(
        forward_block, (split_rows(queries), split_rows(key_proj), split_rows(value_proj))
    ).reshape(rows_here, L, hidden_width)
    gated_out = (gate_act * attended).astype(jnp.bfloat16)
    updated = (
        pair_field
        + jnp.dot(
            gated_out.reshape(rows_here * L, hidden_width),
            w_output,
            preferred_element_type=jnp.float32,
        ).reshape(rows_here, L, C)
        + out_bias
    )
    outgoing = updated.reshape(row_share, tile_grid, tile_grid, tile_count, row_share * C)
    incoming = lax.all_to_all(
        outgoing.astype(jnp.bfloat16), "tile", split_axis=3, concat_axis=3, tiled=True
    ).astype(outgoing.dtype)
    mirrored = (
        incoming.reshape(row_share, tile_grid, tile_grid, tile_count, row_share, C)
        .transpose(4, 2, 1, 3, 0, 5)
        .reshape(rows_here, L, C)
    )
    logits = (
        jnp.einsum("rlc,cb->rlb", updated + mirrored, w_distogram, precision=lax.Precision.HIGHEST)
        + dist_bias
    )
    row_max = jnp.max(logits, axis=-1, keepdims=True)
    exp_logits = jnp.exp(logits - row_max)
    bin_prob = exp_logits / jnp.sum(exp_logits, axis=-1, keepdims=True)
    target_here = targets.reshape(rows_here, L)
    onehot = (target_here[:, :, None] == jnp.arange(NB, dtype=jnp.int32)[None, None, :]).astype(
        jnp.float32
    )
    logit_grad = 2.0 * (bin_prob - onehot)
    pair_grad = jnp.einsum("rlb,cb->rlc", logit_grad, w_distogram, precision=lax.Precision.HIGHEST)
    out_grad = jnp.einsum(
        "rlc,wc->rlw", pair_grad.astype(jnp.bfloat16), w_output, preferred_element_type=jnp.float32
    )
    att_grad_b = (out_grad * gate_act).astype(jnp.bfloat16).reshape(rows_here, L, H, HD)
    gate_grad = out_grad * attended * gate_act * (1.0 - gate_act)

    def backward_block(bias_sum, block_args):
        query_blk, key_blk, value_blk, grad_blk = block_args
        attn_prob = probabilities(query_blk, key_blk, bias_full)
        weights_b = attn_prob.astype(jnp.bfloat16)
        value_grad = jnp.einsum(
            "rhjk,rjhd->rkhd", weights_b, grad_blk, preferred_element_type=jnp.float32
        )
        weight_grad = jnp.einsum(
            "rjhd,rkhd->rhjk", grad_blk, value_blk, preferred_element_type=jnp.float32
        )
        score_grad = attn_prob * (
            weight_grad - jnp.sum(attn_prob * weight_grad, axis=-1, keepdims=True)
        )
        score_b = score_grad.astype(jnp.bfloat16)
        query_grad = (
            jnp.einsum("rhjk,rkhd->rjhd", score_b, key_blk, preferred_element_type=jnp.float32)
            * inv_root
        )
        key_grad = (
            jnp.einsum("rhjk,rjhd->rkhd", score_b, query_blk, preferred_element_type=jnp.float32)
            * inv_root
        )
        return (bias_sum + jnp.sum(score_grad, axis=0), (query_grad, key_grad, value_grad))

    bias_grad, grad_parts = lax.scan(
        backward_block,
        jnp.zeros((H, L, L), jnp.float32),
        (split_rows(queries), split_rows(key_proj), split_rows(value_proj), split_rows(att_grad_b)),
    )
    query_grad, key_grad, value_grad = grad_parts
    owner_order = (
        bias_grad.reshape(H, tile_grid, tile_count, row_share, L)
        .transpose(0, 2, 3, 1, 4)
        .reshape(H, L, L)
    )
    bias_share = lax.psum_scatter(
        owner_order.astype(jnp.bfloat16), "tile", scatter_dimension=1, tiled=True
    ).astype(jnp.float32)

    def back_project(grad_part, weight):
        return jnp.einsum(
            "rlw,cw->rlc",
            grad_part.reshape(rows_here, L, hidden_width).astype(jnp.bfloat16),
            weight,
            preferred_element_type=jnp.float32,
        )

    normed_grad = (
        back_project(query_grad, w_query)
        + back_project(key_grad, w_key)
        + back_project(value_grad, w_value)
        + back_project(gate_grad, w_gate)
    )
    normed_grad = normed_grad + jnp.einsum(
        "hrl,ch->rlc", bias_share, w_pairbias, precision=lax.Precision.HIGHEST
    )
    scaled = normed_grad * ln_gain
    ln_back = inverse * (
        scaled
        - jnp.mean(scaled, axis=-1, keepdims=True)
        - normed * jnp.mean(scaled * normed, axis=-1, keepdims=True)
    )
    total_grad = (pair_grad + ln_back).astype(jnp.bfloat16)
    state_here = lax.axis_index("state")
    piece_cols = L // state_count
    shifted = jnp.roll(total_grad, offsets[state_here], axis=1)
    outgoing_rows = shifted.reshape(rows_here, state_count, piece_cols, C)
    received = lax.all_to_all(outgoing_rows, "state", split_axis=1, concat_axis=1, tiled=True)
    placed = (
        received.astype(jnp.float32)
        .reshape(row_share, tile_grid, state_count, piece_cols, C)
        .transpose(2, 1, 0, 3, 4)
    )
    columns = state_here * piece_cols + jnp.arange(piece_cols, dtype=jnp.int32)
    full_blocks = 2 * tile_grid

    def place(source, accum):
        offset = offsets[source]
        high_half = (columns < offset).astype(jnp.float32)[:, None]
        incoming_blk = lax.dynamic_index_in_dim(placed, source, 0, keepdims=False)
        contrib = jnp.stack([incoming_blk * (1.0 - high_half), incoming_blk * high_half], axis=2)
        row_start = offset // tile_side
        zero_index = jnp.zeros((), jnp.int32)
        corner = (row_start, zero_index, zero_index, zero_index, zero_index)
        window = lax.dynamic_slice(accum, corner, contrib.shape)
        return lax.dynamic_update_slice(accum, window + contrib, corner)

    accum = lax.fori_loop(
        0, state_count, place, jnp.zeros((full_blocks, row_share, 2, piece_cols, C), jnp.float32)
    )
    return accum.reshape(full_blocks, 1, row_share, 2, piece_cols, C)


def solution(mesh):
    in_specs = (
        P("state", "tile", None, None, None),
        P("state", "tile", None, None, None),
        P(),
        P(),
        P(),
        P(),
        P(),
        P(),
        P(),
        P(),
        P(),
        P(),
        P(),
        P(),
        P(),
    )
    out_specs = P(None, "tile", None, None, "state", None)
    return jax.shard_map(
        on_device, mesh=mesh, in_specs=in_specs, out_specs=out_specs, check_vma=False
    )
```

profile of v0, /device:TPU:0, one launch (start us, length us, event | category | flops | bytes accessed | tf_op | source)
XLA Modules:
  0.0 457.8 jit_solution(5351371893127979779)
XLA Ops:
  6.5 4.4 all-to-all-start
  10.9 14.4 %all-to-all-done = bf16[4,16,64,128]{3,2,1,0:T(8,128)(2,1)S(1)} async-done(((bf16[4,16,64,128]{3,2,1,0:T(8,128)(2,1)}), bf16[4,16,64,128]{3,2,1,0:T(8,128)(2,1)S(1)}, u32[]{:S(2)}, u32[]{:S(2)}) %all-to-all-start) | async-done | bytes 1048608 | tf_op jit(solution)/shard_map/all_to_all | solution.py:61
  28.0 3.2 fusion.100
  31.2 5.8 %all_gather.3 = f32[4,128,128]{2,0,1:T(4,128)S(1)} all-gather(f32[4,32,128]{2,0,1:T(4,128)S(1)} %fusion.100), channel_id=1, replica_groups=mesh['state'=8,'tile'=4] {'tile'}, dimensions={1}, use_global_device_ids=true | all-gather | bytes 327680 | tf_op jit(solution)/shard_map/all_gather | solution.py:80
  41.0 2.7 reshape_reshape.15
  43.7 2.6 copy.165
  47.7 2.3 copy.162
  50.0 2.6 reshape_reshape.16
  52.6 2.7 copy.166
  59.6 2.6 copy.167
  62.2 68.6 %while.46 = (s32[]{:T(128)}, f32[16,2,128,4,32]{2,4,3,1,0:T(8,128)}, bf16[16,2,128,4,32]{2,4,3,1,0:T(8,128)(2,1)}, bf16[16,2,128,4,32]{2,4,3,1,0:T(8,128)(2,1)},...) while((s32[]{:T(128)}, f32[16,2,128,4,32]{2,4,3,1,0:T(8,128)}, ...), condition=%wide.region_5.6_spmd.clone, body=%wide.region_2.5_spmd.sunk.clone | while | flops 26346752 | bytes 3091525 | solution.py:94
  130.8 4.5 copy.168
  135.3 3.9 reshape.172
  139.3 3.0 copy.169
  142.3 3.7 multiply_convert_fusion.2
  148.9 2.8 copy.170
  151.7 3.5 all-to-all-start.1
  161.9 2.9 copy.173
  164.8 4.8 %all-to-all-done.1 = bf16[16,2,2,4,2048]{4,0,2,1,3:T(8,128)(2,1)S(1)} async-done(((bf16[16,2,2,4,2048]{4,0,2,1,3:T(8,128)(2,1)}), bf16[16,2,2,4,2048]{4,0,2,1,3:T(8,128)(2,1)S(1)}, u32[]{:S(2)}, u32[]{:S(2)}) %all-to-all-start.1) | async-done | bytes 1048608 | tf_op jit(solution)/shard_map/all_to_all | solution.py:108
  171.8 2.4 fusion.97
  175.7 3.5 fusion.108
  179.2 2.3 multiply_convert_fusion.1
  181.5 155.2 %while.48 = (s32[]{:T(128)}, f32[4,128,128]{1,2,0:T(8,128)}, bf16[16,2,128,4,32]{2,4,3,1,0:T(8,128)(2,1)}, bf16[16,2,128,4,32]{2,4,3,1,0:T(8,128)(2,1)}, bf16[16...) while((s32[]{:T(128)}, f32[4,128,128]{1,2,0:T(8,128)}, ...), condition=%wide.region_13.14_spmd.clone.clone, body=%wide.region_8.13_spmd.clone.sunk.clone | while | flops 52691200 | bytes 6518895 | solution.py:159
  315.2 2.1 fusion.244
  336.7 3.1 fusion.122
  342.8 4.8 %fusion.103 = f32[32,128,128]{2,1,0:T(8,128)} fusion(f32[32,128,128]{1,2,0:T(8,128)} %copy.173, f32[32,128,128]{1,2,0:T(8,128)} %get-tuple-element.441, f32[32,128,128]{1,2,0:T(8,128)} %bitcast.299, bf16[128,128]{1,0:T(8,128)(2,1)S(1)} %copy-done.19), kind=kOutput, calls=%fused_computation.110 | convolution fusion | flops 136839168 | bytes 8421376 | tf_op jit(solution)/shard_map/rlw,cw->rlc/dot_general | solution.py:175
  349.3 26.4 %all-reduce.3.cloned.1.call-done = bf16[4,128,128]{2,0,1:T(4,128)(2,1)} async-done(((bf16[4,128,128]{2,0,1:T(4,128)(2,1)}), bf16[4,128,128]{2,0,1:T(4,128)(2,1)}) %all-reduce.3.cloned.1.call-update) | async-done | bytes 131088
  375.7 5.9 %fusion.137 = (f32[32,128]{1,0:T(8,128)S(1)}, f32[32,128]{1,0:T(8,128)S(1)}, f32[32,128,128]{2,1,0:T(8,128)S(1)}) fusion(f32[32,128]{1,0:T(8,128)S(1)} %rsqrt.17, f32[32,128,128]{2,1,0:T(8,128)S(1)} %bitcast.290, f32[32,128]{1,0:T(8,128)S(1)} %div.57, f32[128]{0:T(128)S(1)} %copy-done.21, f32[128,4]{0,1:T(4,128)S(1)} %copy-done.20, ...), kind=kOutput, calls=%fused_computation.151 | convolution fusion | flops 30400512 | bytes 12683780 | tf_op jit(solution)/shard_map/hrl,ch->rlc/dot_general | solution.py:188
  381.6 2.5 add_convert_fusion
  386.0 5.5 %all-to-all-start.2 = ((bf16[32,8,16,128]{3,2,0,1:T(8,128)(2,1)}), bf16[32,8,16,128]{3,2,0,1:T(8,128)(2,1)S(1)}, u32[]{:S(2)}, u32[]{:S(2)}) async-start(bf16[32,8,16,128]{3,2,0,1:T(8,128)(2,1)} %copy.191), calls=%async_computation.2 | async-start | bytes 2097152 | tf_op jit(solution)/shard_map/all_to_all | solution.py:202
  391.6 24.9 %all-to-all-done.2 = bf16[32,8,16,128]{3,2,0,1:T(8,128)(2,1)S(1)} async-done(((bf16[32,8,16,128]{3,2,0,1:T(8,128)(2,1)}), bf16[32,8,16,128]{3,2,0,1:T(8,128)(2,1)S(1)}, u32[]{:S(2)}, u32[]{:S(2)}) %all-to-all-start.2) | async-done | bytes 1048608 | tf_op jit(solution)/shard_map/all_to_all | solution.py:202
  417.2 32.8 %while.47 = (s32[]{:T(128)}, f32[4,16,2,16,128]{4,3,2,1,0:T(8,128)S(1)}, s32[8]{0:T(128)S(1)}, f32[8,2,16,16,128]{4,3,0,1,2:T(8,128)S(1)}, s32[]{:T(128)}) while((s32[]{:T(128)}, f32[4,16,2,16,128]{4,3,2,1,0:T(8,128)S(1)}, s32[8]{0:T(128)S(1)}, f32[8,2,16,16,128]{4,3,0,1,2:T(8,128)S(1)}, s32[]{:T(128)}) %tuple.139), condition=%wide.region_18.19_spmd.clone.clone, body=%wide.region_17.18_spmd.clone.sunk.clone | while | flops 393300 | bytes 2360721 | solution.py:222
  (324 shorter events, 264.0 us)
Async XLA Ops:
  6.5 139.5 %copy-start = (bf16[128,128]{1,0:T(8,128)(2,1)S(1)}, bf16[128,128]{1,0:T(8,128)(2,1)}, u32[]{:S(2)}) copy-start(bf16[128,128]{1,0:T(8,128)(2,1)} %param.32) | copy-start | bytes 98308
  6.5 18.8 %all-to-all-start = ((bf16[4,16,64,128]{3,2,1,0:T(8,128)(2,1)}), bf16[4,16,64,128]{3,2,1,0:T(8,128)(2,1)S(1)}, u32[]{:S(2)}, u32[]{:S(2)}) async-start(bf16[4,16,64,128]{3,2,1,0:T(8,128)(2,1)} %bitcast.308), calls=%async_computation | async-start | bytes 2097152 | tf_op jit(solution)/shard_map/all_to_all | solution.py:61
  26.1 1.9 copy-start.20
  26.1 1.9 copy-start.21
  26.1 1.9 copy-start.22
  28.0 11.3 %copy-start.14 = (bf16[128,128]{1,0:T(8,128)(2,1)S(1)}, bf16[128,128]{1,0:T(8,128)(2,1)}, u32[]{:S(2)}) copy-start(bf16[128,128]{1,0:T(8,128)(2,1)} %param.28) | copy-start | bytes 98308
  38.3 1.0 copy-start.5
  41.0 5.3 %copy-start.6 = (bf16[4096,128]{1,0:T(8,128)(2,1)S(1)}, bf16[4096,128]{1,0:T(8,128)(2,1)}, u32[]{:S(2)}) copy-start(bf16[4096,128]{1,0:T(8,128)(2,1)} %copy-done.5) | copy-start | bytes 3145732
  41.0 5.3 %copy-start.16 = (bf16[128,128]{1,0:T(8,128)(2,1)S(1)}, bf16[128,128]{1,0:T(8,128)(2,1)}, u32[]{:S(2)}) copy-start(bf16[128,128]{1,0:T(8,128)(2,1)} %param.26) | copy-start | bytes 98308
  50.0 5.2 %copy-start.15 = (bf16[128,128]{1,0:T(8,128)(2,1)S(1)}, bf16[128,128]{1,0:T(8,128)(2,1)}, u32[]{:S(2)}) copy-start(bf16[128,128]{1,0:T(8,128)(2,1)} %param.27) | copy-start | bytes 98308
  139.3 3.0 copy-start.7
  139.3 3.0 copy-start.26
  142.3 3.7 copy-start.23
  151.7 17.9 %all-to-all-start.1 = ((bf16[16,2,2,4,2048]{4,0,2,1,3:T(8,128)(2,1)}), bf16[16,2,2,4,2048]{4,0,2,1,3:T(8,128)(2,1)S(1)}, u32[]{:S(2)}, u32[]{:S(2)}) async-start(bf16[16,2,2,4,2048]{4,0,2,1,3:T(8,128)(2,1)} %copy.170), calls=%async_computation.1 | async-start | bytes 2097152 | tf_op jit(solution)/shard_map/all_to_all | solution.py:108
  155.2 220.5 %all-reduce.3.cloned.1.call-start = ((), (), s32[]{:S(2)}) async-start(), calls=%async_computation.3 | async-start | bytes 262144
  155.7 1.3 copy-start.3
  155.7 2.4 copy-start.27
  155.7 4.9 %copy-start.28 = (u32[32]{0:T(128)S(1)}, u32[32]{0:T(128)}, u32[]{:S(2)}) copy-start(u32[32]{0:T(128)} %constant.184) | copy-start | bytes 388
  170.2 1.6 copy-start.12
  170.2 1.6 copy-start.18
  170.3 1.6 copy-start.24
  174.2 1.5 copy-start.25
  175.7 3.5 copy-start.2
  179.2 2.3 copy-start.10
  336.7 3.1 copy-start.13
  339.9 1.8 copy-start.9
  339.9 2.9 copy-start.19
  342.7 4.8 %copy-start.4 = (bf16[16,2,128,4,32]{2,4,3,1,0:T(8,128)(2,1)S(1)}, bf16[16,2,128,4,32]{2,4,3,1,0:T(8,128)(2,1)}, u32[]{:S(2)}) copy-start(bf16[16,2,128,4,32]{2,4,3,1,0:T(8,128)(2,1)} %get-tuple-element.226) | copy-start | bytes 3145732
  342.7 4.8 %copy-start.17 = (bf16[128,128]{1,0:T(8,128)(2,1)S(1)}, bf16[128,128]{1,0:T(8,128)(2,1)}, u32[]{:S(2)}) copy-start(bf16[128,128]{1,0:T(8,128)(2,1)} %param.26) | copy-start | bytes 98308
  375.7 5.9 %copy-start.11 = (f32[32,128,128]{2,1,0:T(8,128)S(1)}, f32[32,128,128]{2,1,0:T(8,128)}, u32[]{:S(2)}) copy-start(f32[32,128,128]{2,1,0:T(8,128)} %copy-done.10) | copy-start | bytes 6291460
  386.0 30.4 %all-to-all-start.2 = ((bf16[32,8,16,128]{3,2,0,1:T(8,128)(2,1)}), bf16[32,8,16,128]{3,2,0,1:T(8,128)(2,1)S(1)}, u32[]{:S(2)}, u32[]{:S(2)}) async-start(bf16[32,8,16,128]{3,2,0,1:T(8,128)(2,1)} %copy.191), calls=%async_computation.2 | async-start | bytes 2097152 | tf_op jit(solution)/shard_map/all_to_all | solution.py:202
  450.0 1.0 copy-start.8
  (1 other events, 1.0 us)
Sparse Core Ops, SparseCore 0:
  342.8 32.8 all-reduce.2
where the time goes:
time: 466 us; the launch traced here: 458 us
  matrix products  229 us (49%)
  waiting for transfers between devices  70.6 us (15%)
  local copies, waits for them, and re-layouts  57.3 us (12%)
  other arithmetic  43.7 us (9%)
  loops' own time  21.7 us (5%)
  between operations  16.4 us (4%)
  starting transfers between devices  13.6 us (3%)
  blocking collectives  5.78 us (1%)
    sub x32, matrix products, probabilities(): exp_scores = jnp.exp(scores - row_max)  40.1 us
    dot_general x16, matrix products, backward_block(): jnp.einsum('rhjk,rjhd->rkhd', weights_b, grad_blk, preferred_element_type...  32.6 us
    dot_general x16, matrix products, forward_block(): jnp.einsum('rhjk,rkhd->rjhd', weights_b, value_blk, preferred_element_typ...  27.8 us
    dot_general x16, matrix products, backward_block(): jnp.einsum('rhjk,rjhd->rkhd', score_b, query_blk, preferred_element_type=...  27.3 us
    unnamed x2, waiting for transfers between devices  26.4 us
    dot_general x16, matrix products, backward_block(): jnp.einsum('rhjk,rkhd->rjhd', score_b, key_blk, preferred_element_type=jn...  26.4 us
    add x16, other arithmetic, backward_block(): bias_sum + jnp.sum(score_grad, axis=0)  25.9 us
    all_to_all x1, waiting for transfers between devices, on_device(): lax.all_to_all(outgoing_rows, 'state', split_axis=1, concat_axis=1, tiled...  24.9 us
  transfers between devices with their start and end apart: 4, of which 4 were waited for; matrix products, arithmetic and copies ran while one was open for 3% of the time, Pallas kernels for 0%

commit v1 on v0

--- a/solution.py
+++ b/solution.py
@@ -199,7 +199,15 @@
     piece_cols = L // state_count
     shifted = jnp.roll(total_grad, offsets[state_here], axis=1)
     outgoing_rows = shifted.reshape(rows_here, state_count, piece_cols, C)
-    received = lax.all_to_all(outgoing_rows, "state", split_axis=1, concat_axis=1, tiled=True)
+    ways, here = (lax.axis_size("state"), lax.axis_index("state"))
+    width = outgoing_rows.shape[1] // ways
+    turned = jnp.roll(outgoing_rows, -here * width, axis=1)
+    got = [lax.slice_in_dim(turned, 0, width, axis=1)]
+    for far in range(1, ways):
+        sent = lax.slice_in_dim(turned, far * width, (far + 1) * width, axis=1)
+        got.append(lax.ppermute(sent, "state", [(d, (d + far) % ways) for d in range(ways)]))
+    line = jnp.concatenate(got[::-1], axis=1)
+    received = jnp.roll(line, (here + 1) * got[0].shape[1], axis=1)
     placed = (
         received.astype(jnp.float32)
         .reshape(row_share, tile_grid, state_count, piece_cols, C)

time: 466 us -> 459 us (0.985)
  waiting for transfers between devices: 70.6 us -> 63.3 us
    all_to_all x1 -> x0, waiting for transfers between devices: 24.9 us -> none  [on_device(): lax.all_to_all(outgoing_rows, 'state', split_axis=1, concat_axis=1, tiled...]
    ppermute x0 -> x7, waiting for transfers between devices: none -> 17.6 us  [on_device(): lax.ppermute(sent, 'state', [(d, (d + far) % ways) for d in range(ways)])]
    ppermute x0 -> x7, starting transfers between devices: none -> 9.4 us  [on_device(): lax.ppermute(sent, 'state', [(d, (d + far) % ways) for d in range(ways)])]
    all_to_all x1 -> x0, starting transfers between devices: 5.52 us -> none  [on_device(): lax.all_to_all(outgoing_rows, 'state', split_axis=1, concat_axis=1, tiled...]
  transfers between devices with their start and end apart: 4 -> 10, of which waited for: 4 -> 8; matrix products, arithmetic and copies ran while one was open for 3% -> 3% of each run, Pallas kernels for 0% -> 0%
where the time goes in v1:
time: 459 us; the launch traced here: 451 us
  matrix products  229 us (50%)
  waiting for transfers between devices  63.3 us (14%)
  local copies, waits for them, and re-layouts  56.2 us (12%)
  other arithmetic  43.7 us (10%)
  loops' own time  19 us (4%)
  starting transfers between devices  17.5 us (4%)
  between operations  16.4 us (4%)
  blocking collectives  5.78 us (1%)
    sub x32, matrix products, probabilities(): exp_scores = jnp.exp(scores - row_max)  40.1 us
    dot_general x16, matrix products, backward_block(): jnp.einsum('rhjk,rjhd->rkhd', weights_b, grad_blk, preferred_element_type...  32.6 us
    dot_general x16, matrix products, forward_block(): jnp.einsum('rhjk,rkhd->rjhd', weights_b, value_blk, preferred_element_typ...  27.8 us
    dot_general x16, matrix products, backward_block(): jnp.einsum('rhjk,rjhd->rkhd', score_b, query_blk, preferred_element_type=...  27.4 us
    dot_general x16, matrix products, backward_block(): jnp.einsum('rhjk,rkhd->rjhd', score_b, key_blk, preferred_element_type=jn...  26.4 us
    unnamed x2, waiting for transfers between devices  26.4 us
    add x16, other arithmetic, backward_block(): bias_sum + jnp.sum(score_grad, axis=0)  25.8 us
    dot_general x16, matrix products, backward_block(): jnp.einsum('rjhd,rkhd->rhjk', grad_blk, value_blk, preferred_element_type...  18.7 us
  transfers between devices with their start and end apart: 10, of which 8 were waited for; matrix products, arithmetic and copies ran while one was open for 3% of the time, Pallas kernels for 0%

profile of v1, /device:TPU:0, one launch (start us, length us, event | category | flops | bytes accessed | tf_op | source)
XLA Modules:
  0.0 450.9 jit_solution(7825938359700371691)
XLA Ops:
  6.5 4.4 all-to-all-start
  10.9 14.4 %all-to-all-done = bf16[4,16,64,128]{3,2,1,0:T(8,128)(2,1)S(1)} async-done(((bf16[4,16,64,128]{3,2,1,0:T(8,128)(2,1)}), bf16[4,16,64,128]{3,2,1,0:T(8,128)(2,1)S(1)}, u32[]{:S(2)}, u32[]{:S(2)}) %all-to-all-start) | async-done | bytes 1048608 | tf_op jit(solution)/shard_map/all_to_all | solution.py:61
  28.0 3.2 fusion.100
  31.2 5.8 %all_gather.3 = f32[4,128,128]{2,0,1:T(4,128)S(1)} all-gather(f32[4,32,128]{2,0,1:T(4,128)S(1)} %fusion.100), channel_id=1, replica_groups=mesh['state'=8,'tile'=4] {'tile'}, dimensions={1}, use_global_device_ids=true | all-gather | bytes 327680 | tf_op jit(solution)/shard_map/all_gather | solution.py:80
  41.0 2.7 reshape_reshape.15
  43.7 2.6 copy.162
  50.0 2.6 reshape_reshape.16
  52.6 2.7 copy.163
  59.7 2.6 copy.164
  62.3 68.6 %while.46 = (s32[]{:T(128)}, f32[16,2,128,4,32]{2,4,3,1,0:T(8,128)}, bf16[16,2,128,4,32]{2,4,3,1,0:T(8,128)(2,1)}, bf16[16,2,128,4,32]{2,4,3,1,0:T(8,128)(2,1)},...) while((s32[]{:T(128)}, f32[16,2,128,4,32]{2,4,3,1,0:T(8,128)}, ...), condition=%wide.region_5.6_spmd.clone, body=%wide.region_2.5_spmd.sunk.clone | while | flops 26346752 | bytes 3091525 | solution.py:94
  131.0 4.5 %copy.165 = f32[16,2,128,4,32]{2,1,0,4,3:T(2,128)} copy(f32[16,2,128,4,32]{2,4,3,1,0:T(8,128)} %get-tuple-element.226) | data formatting | bytes 4194304 | tf_op jit(solution)/shard_map/while | solution.py:94
  135.5 3.9 reshape.172
  139.4 3.0 copy.166
  142.4 3.7 multiply_convert_fusion.2
  149.0 2.8 copy.167
  151.7 3.5 all-to-all-start.1
  161.9 2.9 copy.170
  164.8 4.9 %all-to-all-done.1 = bf16[16,2,2,4,2048]{4,0,2,1,3:T(8,128)(2,1)S(1)} async-done(((bf16[16,2,2,4,2048]{4,0,2,1,3:T(8,128)(2,1)}), bf16[16,2,2,4,2048]{4,0,2,1,3:T(8,128)(2,1)S(1)}, u32[]{:S(2)}, u32[]{:S(2)}) %all-to-all-start.1) | async-done | bytes 1048608 | tf_op jit(solution)/shard_map/all_to_all | solution.py:108
  171.9 2.4 fusion.97
  175.8 3.5 fusion.110
  179.3 2.3 multiply_convert_fusion.1
  181.6 155.2 %while.48 = (s32[]{:T(128)}, f32[4,128,128]{1,2,0:T(8,128)}, bf16[16,2,128,4,32]{2,4,3,1,0:T(8,128)(2,1)}, bf16[16,2,128,4,32]{2,4,3,1,0:T(8,128)(2,1)}, bf16[16...) while((s32[]{:T(128)}, f32[4,128,128]{1,2,0:T(8,128)}, ...), condition=%wide.region_13.14_spmd.clone.clone, body=%wide.region_8.13_spmd.clone.sunk.clone | while | flops 52691200 | bytes 6518895 | solution.py:159
  336.9 3.1 fusion.124
  342.9 4.8 %fusion.103 = f32[32,128,128]{2,1,0:T(8,128)} fusion(f32[32,128,128]{1,2,0:T(8,128)} %copy.170, f32[32,128,128]{1,2,0:T(8,128)} %get-tuple-element.449, f32[32,128,128]{1,2,0:T(8,128)} %bitcast.299, bf16[128,128]{1,0:T(8,128)(2,1)S(1)} %copy-done.19), kind=kOutput, calls=%fused_computation.114 | convolution fusion | flops 136839168 | bytes 8421376 | tf_op jit(solution)/shard_map/rlw,cw->rlc/dot_general | solution.py:175
  349.5 26.4 %all-reduce.3.cloned.1.call-done = bf16[4,128,128]{2,0,1:T(4,128)(2,1)} async-done(((bf16[4,128,128]{2,0,1:T(4,128)(2,1)}), bf16[4,128,128]{2,0,1:T(4,128)(2,1)}) %all-reduce.3.cloned.1.call-update) | async-done | bytes 131088
  375.8 5.9 %fusion.139 = (f32[32,128]{1,0:T(8,128)S(1)}, f32[32,128]{1,0:T(8,128)S(1)}, f32[32,128,128]{2,1,0:T(8,128)S(1)}) fusion(f32[32,128]{1,0:T(8,128)S(1)} %rsqrt.17, f32[32,128,128]{2,1,0:T(8,128)S(1)} %bitcast.290, f32[32,128]{1,0:T(8,128)S(1)} %div.57, f32[128]{0:T(128)S(1)} %copy-done.21, f32[128,4]{0,1:T(4,128)S(1)} %copy-done.20, ...), kind=kOutput, calls=%fused_computation.165 | convolution fusion | flops 30400512 | bytes 12683780 | tf_op jit(solution)/shard_map/hrl,ch->rlc/dot_general | solution.py:188
  381.7 2.5 add_convert_fusion
  385.6 4.3 collective-permute-start
  390.4 2.9 collective-permute-start.3
  396.6 2.7 collective-permute-done.2
  399.4 11.9 %collective-permute-done.3 = bf16[32,1,16,128]{3,2,1,0:T(8,128)(2,1)S(1)} collective-permute-done((bf16[32,1,16,128]{3,2,1,0:T(8,128)(2,1)S(1)}, bf16[32,1,16,128]{3,2,1,0:T(8,128)(2,1)S(1)}, u32[]{:S(2)}, u32[]{:S(2)}) %collective-permute-start.3) | collective-permute-done | bytes 131104 | tf_op jit(solution)/shard_map/ppermute | solution.py:208
  413.6 29.5 %while.47 = (s32[]{:T(128)}, f32[4,16,2,16,128]{4,3,2,1,0:T(8,128)S(1)}, s32[8]{0:T(128)S(1)}, f32[8,2,16,16,128]{4,3,0,1,2:T(8,128)S(1)}, s32[]{:T(128)}) while((s32[]{:T(128)}, f32[4,16,2,16,128]{4,3,2,1,0:T(8,128)S(1)}, s32[8]{0:T(128)S(1)}, f32[8,2,16,16,128]{4,3,0,1,2:T(8,128)S(1)}, s32[]{:T(128)}) %tuple.146), condition=%wide.region_18.20_spmd.clone.clone, body=%wide.region_17.19_spmd.clone.sunk.clone | while | flops 393300 | bytes 2360721 | solution.py:230
  (345 shorter events, 272.6 us)
Async XLA Ops:
  6.5 139.6 %copy-start = (bf16[128,128]{1,0:T(8,128)(2,1)S(1)}, bf16[128,128]{1,0:T(8,128)(2,1)}, u32[]{:S(2)}) copy-start(bf16[128,128]{1,0:T(8,128)(2,1)} %param.34) | copy-start | bytes 98308
  6.5 18.8 %all-to-all-start = ((bf16[4,16,64,128]{3,2,1,0:T(8,128)(2,1)}), bf16[4,16,64,128]{3,2,1,0:T(8,128)(2,1)S(1)}, u32[]{:S(2)}, u32[]{:S(2)}) async-start(bf16[4,16,64,128]{3,2,1,0:T(8,128)(2,1)} %bitcast.308), calls=%async_computation | async-start | bytes 2097152 | tf_op jit(solution)/shard_map/all_to_all | solution.py:61
  26.1 1.9 copy-start.20
  26.1 1.9 copy-start.21
  26.1 1.9 copy-start.22
  28.0 11.3 %copy-start.14 = (bf16[128,128]{1,0:T(8,128)(2,1)S(1)}, bf16[128,128]{1,0:T(8,128)(2,1)}, u32[]{:S(2)}) copy-start(bf16[128,128]{1,0:T(8,128)(2,1)} %param.30) | copy-start | bytes 98308
  41.0 5.3 %copy-start.6 = (bf16[4096,128]{1,0:T(8,128)(2,1)S(1)}, bf16[4096,128]{1,0:T(8,128)(2,1)}, u32[]{:S(2)}) copy-start(bf16[4096,128]{1,0:T(8,128)(2,1)} %copy-done.5) | copy-start | bytes 3145732
  41.0 5.3 %copy-start.16 = (bf16[128,128]{1,0:T(8,128)(2,1)S(1)}, bf16[128,128]{1,0:T(8,128)(2,1)}, u32[]{:S(2)}) copy-start(bf16[128,128]{1,0:T(8,128)(2,1)} %param.28) | copy-start | bytes 98308
  50.0 5.3 %copy-start.15 = (bf16[128,128]{1,0:T(8,128)(2,1)S(1)}, bf16[128,128]{1,0:T(8,128)(2,1)}, u32[]{:S(2)}) copy-start(bf16[128,128]{1,0:T(8,128)(2,1)} %param.29) | copy-start | bytes 98308
  139.4 3.0 copy-start.7
  139.4 3.0 copy-start.26
  142.4 3.7 copy-start.23
  151.7 17.9 %all-to-all-start.1 = ((bf16[16,2,2,4,2048]{4,0,2,1,3:T(8,128)(2,1)}), bf16[16,2,2,4,2048]{4,0,2,1,3:T(8,128)(2,1)S(1)}, u32[]{:S(2)}, u32[]{:S(2)}) async-start(bf16[16,2,2,4,2048]{4,0,2,1,3:T(8,128)(2,1)} %copy.167), calls=%async_computation.1 | async-start | bytes 2097152 | tf_op jit(solution)/shard_map/all_to_all | solution.py:108
  155.3 220.5 %all-reduce.3.cloned.1.call-start = ((), (), s32[]{:S(2)}) async-start(), calls=%async_computation.2 | async-start | bytes 262144
  155.7 2.4 copy-start.27
  155.8 4.9 %copy-start.28 = (u32[32]{0:T(128)S(1)}, u32[32]{0:T(128)}, u32[]{:S(2)}) copy-start(u32[32]{0:T(128)} %constant.201) | copy-start | bytes 388
  170.3 1.6 copy-start.12
  175.8 3.5 copy-start.2
  179.3 2.3 copy-start.10
  336.8 3.2 copy-start.13
  340.0 1.8 copy-start.9
  340.0 2.9 copy-start.19
  342.9 4.8 %copy-start.4 = (bf16[16,2,128,4,32]{2,4,3,1,0:T(8,128)(2,1)S(1)}, bf16[16,2,128,4,32]{2,4,3,1,0:T(8,128)(2,1)}, u32[]{:S(2)}) copy-start(bf16[16,2,128,4,32]{2,4,3,1,0:T(8,128)(2,1)} %get-tuple-element.227) | copy-start | bytes 3145732
  342.9 4.8 %copy-start.17 = (bf16[128,128]{1,0:T(8,128)(2,1)S(1)}, bf16[128,128]{1,0:T(8,128)(2,1)}, u32[]{:S(2)}) copy-start(bf16[128,128]{1,0:T(8,128)(2,1)} %param.28) | copy-start | bytes 98308
  375.8 5.9 %copy-start.11 = (f32[32,128,128]{2,1,0:T(8,128)S(1)}, f32[32,128,128]{2,1,0:T(8,128)}, u32[]{:S(2)}) copy-start(f32[32,128,128]{2,1,0:T(8,128)} %copy-done.10) | copy-start | bytes 6291460
  385.6 8.2 %collective-permute-start = (bf16[32,1,16,128]{3,2,1,0:T(8,128)(2,1)S(1)}, bf16[32,1,16,128]{3,2,1,0:T(8,128)(2,1)S(1)}, u32[]{:S(2)}, u32[]{:S(2)}) collective-permute-start(bf16[32,1,16,128]{3,2,1,0:T(8,128)(2,1)S(1)} %get-tuple-element.441), channel_id=1, source_target_pairs={{0,28},{4,0},{8,4},{12,8},{16,12},{20,16},{24,20},{28,24},{1,29},{... | collective-permute-start | bytes 393224 | tf_op jit(solution)/shard_map/ppermute | solution.py:208
  389.9 6.7 %collective-permute-start.1 = (bf16[32,1,16,128]{3,2,1,0:T(8,128)(2,1)S(1)}, bf16[32,1,16,128]{3,2,1,0:T(8,128)(2,1)S(1)}, u32[]{:S(2)}, u32[]{:S(2)}) collective-permute-start(bf16[32,1,16,128]{3,2,1,0:T(8,128)(2,1)S(1)} %get-tuple-element.440), channel_id=1, source_target_pairs={{0,24},{4,28},{8,0},{12,4},{16,8},{20,12},{24,16},{28,20},{1,25},{... | collective-permute-start | bytes 393224 | tf_op jit(solution)/shard_map/ppermute | solution.py:208
  390.4 9.0 %collective-permute-start.2 = (bf16[32,1,16,128]{3,2,1,0:T(8,128)(2,1)S(1)}, bf16[32,1,16,128]{3,2,1,0:T(8,128)(2,1)S(1)}, u32[]{:S(2)}, u32[]{:S(2)}) collective-permute-start(bf16[32,1,16,128]{3,2,1,0:T(8,128)(2,1)S(1)} %get-tuple-element.439), channel_id=1, source_target_pairs={{0,20},{4,24},{8,28},{12,0},{16,4},{20,8},{24,12},{28,16},{1,21},{... | collective-permute-start | bytes 393224 | tf_op jit(solution)/shard_map/ppermute | solution.py:208
  390.4 20.9 %collective-permute-start.3 = (bf16[32,1,16,128]{3,2,1,0:T(8,128)(2,1)S(1)}, bf16[32,1,16,128]{3,2,1,0:T(8,128)(2,1)S(1)}, u32[]{:S(2)}, u32[]{:S(2)}) collective-permute-start(bf16[32,1,16,128]{3,2,1,0:T(8,128)(2,1)S(1)} %get-tuple-element.438), channel_id=1, source_target_pairs={{0,16},{4,20},{8,24},{12,28},{16,0},{20,4},{24,8},{28,12},{1,17},{... | collective-permute-start | bytes 393224 | tf_op jit(solution)/shard_map/ppermute | solution.py:208
  393.3 19.3 %collective-permute-start.4 = (bf16[32,1,16,128]{3,2,1,0:T(8,128)(2,1)S(1)}, bf16[32,1,16,128]{3,2,1,0:T(8,128)(2,1)S(1)}, u32[]{:S(2)}, u32[]{:S(2)}) collective-permute-start(bf16[32,1,16,128]{3,2,1,0:T(8,128)(2,1)S(1)} %get-tuple-element.437), channel_id=1, source_target_pairs={{0,12},{4,16},{8,20},{12,24},{16,28},{20,0},{24,4},{28,8},{1,13},{... | collective-permute-start | bytes 393224 | tf_op jit(solution)/shard_map/ppermute | solution.py:208
  393.8 19.0 %collective-permute-start.5 = (bf16[32,1,16,128]{3,2,1,0:T(8,128)(2,1)S(1)}, bf16[32,1,16,128]{3,2,1,0:T(8,128)(2,1)S(1)}, u32[]{:S(2)}, u32[]{:S(2)}) collective-permute-start(bf16[32,1,16,128]{3,2,1,0:T(8,128)(2,1)S(1)} %get-tuple-element.436), channel_id=1, source_target_pairs={{0,8},{4,12},{8,16},{12,20},{16,24},{20,28},{24,0},{28,4},{1,9},{5... | collective-permute-start | bytes 393224 | tf_op jit(solution)/shard_map/ppermute | solution.py:208
  396.6 16.2 %collective-permute-start.6 = (bf16[32,1,16,128]{3,2,1,0:T(8,128)(2,1)S(1)}, bf16[32,1,16,128]{3,2,1,0:T(8,128)(2,1)S(1)}, u32[]{:S(2)}, u32[]{:S(2)}) collective-permute-start(bf16[32,1,16,128]{3,2,1,0:T(8,128)(2,1)S(1)} %get-tuple-element.435), channel_id=1, source_target_pairs={{0,4},{4,8},{8,12},{12,16},{16,20},{20,24},{24,28},{28,0},{1,5},{5... | collective-permute-start | bytes 393224 | tf_op jit(solution)/shard_map/ppermute | solution.py:208
  (7 other events, 8.9 us)
Sparse Core Ops, SparseCore 0:
  343.0 32.7 all-reduce.2
